TPU v7x, 32 devices: a whole 2x2x4 slice. The times are simulated.
32 devices in a mesh: cell: 8 (over z, y), grp: 4 (over x, core).
Axes of the slice: x: 2, y: 2, z: 4, core: 2. Of those that a mesh axis runs over, the one named last changes fastest.
Arguments:
- initial_guess: float32 [9, 6144], P(None, 'cell'), may hold values from -3 to 3
- right_side: float32 [9, 6144], P(None, 'cell')
- camera_blocks: float32 [9, 9, 6144], P(None, None, 'cell'), as said below
- point_inverse: float32 [3, 3, 16384], P(None, None, ('cell', 'grp')), as said below
- jacobian_tiles: bfloat16 [192, 576, 384], P(('cell', 'grp'))
- tile_pattern: int32 [192, 2], P(('cell', 'grp')), may hold values from 0 to 35, as said below
- cell_load: int32 [8], P('cell'), may hold values from 2 to 6, as said below
Outputs:
- solution: float32 [9, 6144], P(None, 'cell')
- residual: float32 [9, 6144], P(None, 'cell')
Inputs may be any that keep to these rules, and one draw needn't show every extreme that they name: `tile_pattern`: column 0 is below 36, column 1 below 4. `cell_load`: A quarter of the cells, rounded down, chosen from the seed, have 6 live slots on each of their devices; every other cell has 2. Slots at or past the load are unused. `camera_blocks`: each camera block is symmetric with a dominant diagonal. `point_inverse`: each point's block is symmetric with a dominant diagonal.
All inputs are finite; a program needn't handle non-finite values.
Results may differ from a plain program's by a relative error of at most 0.0095.
Values may be sent and summed in bfloat16 or wider, within the bound.
A program may use at most 64 MiB of HBM per device.

v0:
```python
import functools

import jax
import jax.numpy as jnp
from jax import lax
from jax.experimental import pallas as pl
from jax.experimental.pallas import tpu as pltpu
from jax.sharding import PartitionSpec as P

CAM_TILE = 64
ITERS = 2
REACH = 2
SPAN = 2 * REACH + 1
ORDER = sorted(range(-REACH, REACH + 1), key=abs)
LANES = 128
ROWS = 8
MESH = pl.DeviceIdType.MESH
F32 = jnp.float32
BF16 = jnp.bfloat16


def kernel(
    cells,
    grps,
    guess_hbm,
    right_hbm,
    blocks_hbm,
    inverse_hbm,
    jac_hbm,
    pattern,
    load,
    solution_ref,
    residual_ref,
    guess,
    right,
    blocks,
    inverse,
    jac,
    window,
    guess_send,
    guess_recv,
    halo_send,
    halo_recv,
    image_send,
    image_recv,
    pattern_send,
    pattern_recv,
    slot_send,
    slot_recv,
    scalar_send,
    scalar_recv,
    local_sem,
    jac_sem,
    halo_send_sem,
    halo_recv_sem,
    image_send_sem,
    image_recv_sem,
    pattern_sem,
    slot_send_sem,
    slot_recv_sem,
    scalar_sem,
):
    params, cameras = guess.shape
    slots, rows_wide, points_wide = jac.shape
    tiles = cameras // CAM_TILE
    pairs = cameras // LANES
    coords = inverse.shape[0]
    point_tiles = inverse.shape[2] // LANES
    devices = cells * grps
    cell = lax.axis_index("cell")
    grp = lax.axis_index("grp")

    local = [
        pltpu.make_async_copy(src, dst, local_sem.at[i])
        for i, (src, dst) in enumerate(
            ((guess_hbm, guess), (blocks_hbm, blocks), (right_hbm, right), (inverse_hbm, inverse))
        )
    ]
    jac_copies = [
        pltpu.make_async_copy(jac_hbm.at[s], jac.at[s], jac_sem.at[s]) for s in range(slots)
    ]
    for copy in local:
        copy.start()
    for copy in jac_copies:
        copy.start()

    barrier = pltpu.get_barrier_semaphore()

    turned = [lax.rem(grp + turn, grps) for turn in range(grps)]

    def everyone(act):
        for turn in range(1, grps):
            act(turn - 1, (cell, turned[turn]))

        def one_cell(delta, carry):
            other = lax.rem(cell + delta, cells)
            for turn in range(grps):
                act(delta * grps + (turn - 1), (other, turned[turn]))
            return carry

        lax.fori_loop(1, cells, one_cell, 0)

    def greet(index, device):
        pl.semaphore_signal(barrier, inc=1, device_id=device, device_id_type=MESH)

    everyone(greet)

    def near(delta, turn):
        return (lax.rem(cell + delta + cells, cells), lax.rem(grp + turn, grps))

    def slot_index(delta, turn):
        return ORDER.index(delta) * grps + turn % grps

    def peers(reach):
        found = []
        for delta in sorted(range(-reach, reach + 1), key=abs):
            for turn in range(grps):
                if delta != 0 or turn != 0:
                    found.append((delta, turn))
        return sorted(found, key=lambda peer: (abs(peer[0]), -peer[1]))

    def iota(shape, axis):
        return lax.broadcasted_iota(jnp.int32, shape, axis)

    lane8 = iota((ROWS, LANES), 1)
    row8 = iota((ROWS, LANES), 0)
    lane9 = iota((params, LANES), 1)
    row9 = iota((params, LANES), 0)
    low9 = lane9 < CAM_TILE
    chunks = (rows_wide + LANES - 1) // LANES
    own_rows = [row9 == 2 * b + (lane9 >= CAM_TILE).astype(jnp.int32) for b in range(chunks)]

    live = [s < load[0] for s in range(slots)]
    ids = [pattern[0, s] for s in range(slots)]
    point_ids = [pattern[1, s] for s in range(slots)]
    id_rows = jnp.full((ROWS, LANES), -4096, jnp.int32)
    point_rows = jnp.full((ROWS, LANES), -1, jnp.int32)
    for s in range(slots):
        id_rows = jnp.where(row8 == s, jnp.where(live[s], ids[s], -4096), id_rows)
        point_rows = jnp.where(row8 == s, point_ids[s], point_rows)
    pattern_send[...] = id_rows
    pattern_recv[0] = id_rows

    def pack(field):
        tail = jnp.zeros((ROWS, LANES), F32)
        for i in range(pairs):
            tail = jnp.where(row8 == i, field[ROWS:, i * LANES : (i + 1) * LANES], tail)
        return jnp.concatenate([field[:ROWS], tail], axis=1)

    def unpack(packed):
        return [
            jnp.concatenate(
                [packed[:, i * LANES : (i + 1) * LANES], packed[i : i + 1, cameras:]], axis=0
            )
            for i in range(pairs)
        ]

    def blocks_of(field):
        return [field[:, i * LANES : (i + 1) * LANES] for i in range(pairs)]

    local[0].wait()
    guess_send[...] = pack(guess[...]).astype(BF16)
    local[1].wait()

    def block_product(field):
        total = blocks[0] * field[0:1, :]
        for k in range(1, params):
            total = total + blocks[k] * field[k : k + 1, :]
        return total

    row_wide = iota((params, cameras), 0)
    diagonal = blocks[0]
    for k in range(1, params):
        diagonal = jnp.where(row_wide == k, blocks[k], diagonal)
    scale = 1.0 / diagonal
    local[2].wait()
    residual0 = right[...] - block_product(guess[...])
    halo_send[0] = pack(residual0 * scale)
    halo_send[1] = pack(scale)
    local[3].wait()
    inverse_rows = []
    for j in range(coords):
        for i in range(coords):
            picked = jnp.zeros((ROWS, LANES), F32)
            for q in range(point_tiles):
                picked = jnp.where(
                    point_rows == q, inverse[j, i : i + 1, q * LANES : (q + 1) * LANES], picked
                )
            inverse_rows.append(picked)
    pad = jnp.zeros((ROWS, chunks * LANES - rows_wide), F32)

    pl.semaphore_wait(barrier, devices - 1)

    halo_copies = []
    for part in range(3):
        for side, delta in ((0, 1), (1, -1)):
            copy = pltpu.make_async_remote_copy(
                src_ref=guess_send if part == 0 else halo_send.at[part - 1],
                dst_ref=guess_recv.at[side] if part == 0 else halo_recv.at[side, part - 1],
                send_sem=halo_send_sem.at[side, part],
                recv_sem=halo_recv_sem.at[side, part],
                device_id=near(delta, 0),
                device_id_type=MESH,
            )
            halo_copies.append(copy)
    halo_copies[0].start()
    halo_copies[1].start()
    for delta, turn in peers(REACH):
        pltpu.make_async_remote_copy(
            src_ref=pattern_send,
            dst_ref=pattern_recv.at[slot_index(-delta, -turn)],
            send_sem=pattern_sem.at[0],
            recv_sem=pattern_sem.at[1],
            device_id=near(delta, turn),
            device_id_type=MESH,
        ).start()
    for copy in halo_copies[2:]:
        copy.start()

    def put(side, parts):
        for i in range(pairs):
            window[side * pairs + i] = parts[i]

    def slot_rows():
        forward = jnp.zeros((ROWS, points_wide), F32)
        row_points = iota((ROWS, points_wide), 0)
        for s in range(slots):
            block = window[lax.shift_right_logical(ids[s], 1)]
            turned = pltpu.roll(block, CAM_TILE, 1)
            odd = lax.bitwise_and(ids[s], 1)
            keep = jnp.where(low9, 0, 1) == odd
            tile = jnp.where(keep, block, turned)
            tile = jnp.where(live[s], tile, 0.0)
            spread = jnp.concatenate([jnp.where(own, tile, 0.0) for own in own_rows], axis=1)
            left = spread[:, :rows_wide].astype(BF16)
            product = jnp.dot(left, jac[s], preferred_element_type=F32)
            total = jnp.sum(product, axis=0, keepdims=True)
            forward = jnp.where(row_points == s, total, forward)
        wide_points = jnp.concatenate([point_rows] * coords, axis=1)
        sums = jnp.zeros((ROWS, points_wide), F32)
        for s in range(slots):
            sums = sums + jnp.where(wide_points == point_ids[s], forward[s : s + 1, :], 0.0)
        solved = []
        for j in range(coords):
            total = inverse_rows[j * coords] * sums[:, :LANES]
            for i in range(1, coords):
                total = total + inverse_rows[j * coords + i] * sums[:, i * LANES : (i + 1) * LANES]
            solved.append(total)
        solved = jnp.concatenate(solved, axis=1).astype(BF16)
        energy = forward * solved.astype(F32)
        backward = jnp.zeros((ROWS, rows_wide), F32)
        row_cams = iota((ROWS, rows_wide), 0)
        for s in range(slots):
            product = lax.dot_general(
                solved, jac[s], (((1,), (1,)), ((), ())), preferred_element_type=F32
            )
            backward = jnp.where(row_cams == s, jnp.where(live[s], product, 0.0), backward)
        backward = jnp.concatenate([backward, pad], axis=1).astype(BF16)
        energy_lanes = energy[:, :LANES]
        for i in range(1, coords):
            energy_lanes = energy_lanes + energy[:, i * LANES : (i + 1) * LANES]
        return backward, jnp.sum(energy_lanes, axis=0, keepdims=True)

    def send_slots(turn_no, backward, reach):
        slot_send[turn_no] = backward
        slot_recv[turn_no, 0] = backward
        for delta, turn in peers(reach):
            pltpu.make_async_remote_copy(
                src_ref=slot_send.at[turn_no],
                dst_ref=slot_recv.at[turn_no, slot_index(-delta, -turn)],
                send_sem=slot_send_sem.at[turn_no],
                recv_sem=slot_recv_sem.at[turn_no],
                device_id=near(delta, turn),
                device_id_type=MESH,
            ).start()

    others = pl.ds(1, SPAN * grps - 1)
    closer = pl.ds(1, 3 * grps - 1)

    def wait_bytes(ref, sem):
        pltpu.make_async_copy(ref, ref, sem).wait()

    def gather_back(turn_no, chooser, sides, count):
        wait_bytes(slot_recv.at[turn_no, pl.ds(1, count - 1)], slot_recv_sem.at[turn_no])
        height = count * ROWS
        stacked = slot_recv[turn_no, :count].astype(F32).reshape(height, chunks * LANES)
        summed = jnp.dot(
            chooser[:, :height], stacked.astype(BF16), preferred_element_type=F32
        )
        fields = []
        for side in sides:
            parts = []
            for i in range(pairs):
                first = side * tiles + 2 * i
                both = []
                for t in (first, first + 1):
                    total = jnp.zeros((params, LANES), F32)
                    for b in range(chunks):
                        piece = summed[t : t + 1, b * LANES : (b + 1) * LANES]
                        total = jnp.where(own_rows[b], piece, total)
                    both.append(total)
                parts.append(
                    jnp.where(low9, both[0], both[1])
                    + pltpu.roll(jnp.where(low9, both[1], both[0]), CAM_TILE, 1)
                )
            fields.append(parts)
        return fields

    put(1, blocks_of(guess[...]))
    halo_copies[0].wait()
    halo_copies[1].wait()
    put(0, unpack(guess_recv[0].astype(F32)))
    put(2, unpack(guess_recv[1].astype(F32)))
    for copy in jac_copies:
        copy.wait()
    backward, _ = slot_rows()
    send_slots(0, backward, REACH)

    wait_bytes(pattern_recv.at[others], pattern_sem.at[1])
    columns = []
    for shift, delta in enumerate(ORDER):
        for turn in range(grps):
            at = pattern_recv[shift * grps + turn] + delta * tiles
            columns.append((at == lane8).astype(F32))
    chosen = jnp.concatenate(columns, axis=0).astype(BF16)
    unit = (iota((LANES, LANES), 0) == iota((LANES, LANES), 1)).astype(F32).astype(BF16)
    chooser = lax.dot_general(
        unit, chosen, (((1,), (1,)), ((), ())), preferred_element_type=F32
    )[: 3 * tiles].astype(BF16)
    for copy in halo_copies[2:]:
        copy.wait()

    left, own, right_side = gather_back(0, chooser, (0, 1, 2), SPAN * grps)
    residual0 = residual0 + jnp.concatenate(own, axis=1)
    direction = residual0 * scale
    put(1, blocks_of(direction))
    scales = [unpack(halo_recv[side, 1]) for side in (0, 1)]
    directions = [
        [
            start + factor * back
            for start, factor, back in zip(unpack(halo_recv[side, 0]), scales[side], backs)
        ]
        for side, backs in ((0, left), (1, right_side))
    ]
    put(0, directions[0])
    put(2, directions[1])
    product1 = block_product(direction)
    image_send[...] = pack(product1 * scale)
    image_copies = []
    for side, delta in ((0, 1), (1, -1)):
        copy = pltpu.make_async_remote_copy(
            src_ref=image_send,
            dst_ref=image_recv.at[side],
            send_sem=image_send_sem.at[side],
            recv_sem=image_recv_sem.at[side],
            device_id=near(delta, 0),
            device_id_type=MESH,
        )
        copy.start()
        image_copies.append(copy)
    backward, _ = slot_rows()
    send_slots(1, backward, REACH)
    for copy in image_copies:
        copy.wait()
    left, own, right_side = gather_back(1, chooser, (0, 1, 2), SPAN * grps)
    image1 = product1 - jnp.concatenate(own, axis=1)
    trial = residual0 - image1
    shaped = trial * scale
    put(1, blocks_of(shaped))
    for side, backs in ((0, left), (1, right_side)):
        put(
            2 * side,
            [
                start - image + factor * back
                for start, image, factor, back in zip(
                    directions[side], unpack(image_recv[side]), scales[side], backs
                )
            ],
        )
    backward, energy = slot_rows()
    send_slots(2, backward, 1)
    product2 = block_product(shaped)

    def lane_sum(field):
        total = field[:, :LANES]
        for i in range(1, pairs):
            total = total + field[:, i * LANES : (i + 1) * LANES]
        return jnp.sum(total, axis=0, keepdims=True) * (1.0 / grps)

    sums = jnp.zeros((ROWS, LANES), F32)
    for i, value in enumerate(
        (
            lane_sum(residual0 * direction),
            lane_sum(direction * image1),
            lane_sum(residual0 * shaped),
            lane_sum(trial * shaped),
            lane_sum(image1 * shaped),
            lane_sum(shaped * product2) - energy,
        )
    ):
        sums = jnp.where(row8 == i, value, sums)
    scalar_send[...] = sums

    def send_scalars(index, device):
        pltpu.make_async_remote_copy(
            src_ref=scalar_send,
            dst_ref=scalar_recv.at[index],
            send_sem=scalar_sem.at[0],
            recv_sem=scalar_sem.at[1],
            device_id=device,
            device_id_type=MESH,
        ).start()

    everyone(send_scalars)
    (own,) = gather_back(2, chooser, (1,), 3 * grps)
    image2 = product2 - jnp.concatenate(own, axis=1)
    wait_bytes(scalar_recv, scalar_sem.at[1])
    totals = jnp.sum(sums + jnp.sum(scalar_recv[...], axis=0), axis=1, keepdims=True)
    rz0, curve1, cross, trial_rz, mixed, curve_w = [totals[i : i + 1, :] for i in range(6)]
    step1 = rz0 / curve1
    short = 1.0 - step1
    rz1 = short * short * rz0 + 2.0 * short * step1 * cross + step1 * step1 * trial_rz
    keep = short + rz1 / rz0
    curve2 = keep * keep * curve1 + 2.0 * keep * step1 * mixed + step1 * step1 * curve_w
    step2 = rz1 / curve2
    near_part = step1 + step2 * keep
    far_part = step2 * step1
    solution_ref[...] = guess[...] + near_part * direction + far_part * shaped
    residual_ref[...] = residual0 - near_part * image1 - far_part * image2

    wait_bytes(scalar_recv, scalar_sem.at[0])
    wait_bytes(pattern_recv.at[others], pattern_sem.at[0])
    for turn_no, sent in enumerate((others, others, closer)):
        wait_bytes(slot_recv.at[turn_no, sent], slot_send_sem.at[turn_no])


def finish_kernel(first, second, solution_ref, residual_ref):
    solution_ref[...] = first[...]
    residual_ref[...] = second[...]


def finish(first, second):
    vmem = pl.BlockSpec(memory_space=pltpu.VMEM)
    shape = jax.ShapeDtypeStruct(first.shape, first.dtype)
    return pl.pallas_call(
        finish_kernel, out_shape=(shape, shape), in_specs=[vmem] * 2, out_specs=(vmem, vmem)
    )(first, second)


def per_device(
    cells, grps, initial_guess, right_side, camera_blocks, point_inverse, jacobian_tiles, tile_pattern, cell_load
):
    params, cameras = initial_guess.shape
    slots, rows_wide, points_wide = jacobian_tiles.shape
    chunks = (rows_wide + LANES - 1) // LANES
    near = SPAN * grps
    packed = cameras + LANES
    hbm = pl.BlockSpec(memory_space=pl.ANY)
    smem = pl.BlockSpec(memory_space=pltpu.SMEM)
    vmem = pl.BlockSpec(memory_space=pltpu.VMEM)
    dma = pltpu.SemaphoreType.DMA
    field = jax.ShapeDtypeStruct((params, cameras), F32)
    first, second = pl.pallas_call(
        functools.partial(kernel, cells, grps),
        out_shape=(field, field),
        in_specs=[hbm] * 5 + [smem] * 2,
        out_specs=(vmem, vmem),
        scratch_shapes=[
            pltpu.VMEM((params, cameras), F32),
            pltpu.VMEM((params, cameras), F32),
            pltpu.VMEM(camera_blocks.shape, F32),
            pltpu.VMEM(point_inverse.shape, F32),
            pltpu.VMEM(jacobian_tiles.shape, BF16),
            pltpu.VMEM((3 * cameras // LANES, params, LANES), F32),
            pltpu.VMEM((ROWS, packed), BF16),
            pltpu.VMEM((2, ROWS, packed), BF16),
            pltpu.VMEM((2, ROWS, packed), F32),
            pltpu.VMEM((2, 2, ROWS, packed), F32),
            pltpu.VMEM((ROWS, packed), F32),
            pltpu.VMEM((2, ROWS, packed), F32),
            pltpu.VMEM((ROWS, LANES), jnp.int32),
            pltpu.VMEM((near, ROWS, LANES), jnp.int32),
            pltpu.VMEM((3, ROWS, chunks * LANES), BF16),
            pltpu.VMEM((3, near, ROWS, chunks * LANES), BF16),
            pltpu.VMEM((ROWS, LANES), F32),
            pltpu.VMEM((cells * grps - 1, ROWS, LANES), F32),
            dma((4,)),
            dma((slots,)),
            dma((2, 3)),
            dma((2, 3)),
            dma((2,)),
            dma((2,)),
            dma((2,)),
            dma((3,)),
            dma((3,)),
            dma((2,)),
        ],
        compiler_params=pltpu.CompilerParams(collective_id=0, has_side_effects=True),
    )(initial_guess, right_side, camera_blocks, point_inverse, jacobian_tiles, tile_pattern.T, cell_load)
    return finish(first, second)


def solution(mesh):
    placed = (
        P(None, "cell"),
        P(None, "cell"),
        P(None, None, "cell"),
        P(None, None, ("cell", "grp")),
        P(("cell", "grp"), None, None),
        P(("cell", "grp"), None),
        P("cell"),
    )
    return jax.shard_map(
        functools.partial(per_device, mesh.shape["cell"], mesh.shape["grp"]),
        mesh=mesh,
        in_specs=placed,
        out_specs=(P(None, "cell"), P(None, "cell")),
        check_vma=False,
    )
```

profile of v0, /device:TPU:0, one launch (start us, length us, event | category | flops | bytes accessed | tf_op | source)
XLA Modules:
  0.0 35.6 jit_solution(7557824908289096616)
XLA Ops:
  1.3 32.8 %shard_map.86 = (f32[9,768]{1,0:T(8,128)}, f32[9,768]{1,0:T(8,128)}) custom-call(f32[9,768]{1,0:T(8,128)} %guess_hbm.1, f32[9,768]{1,0:T(8,128)} %right_hbm.1, f32[9,9,768]{2,1,0:T(8,128)} %blocks_hbm.1, f32[3,3,512]{2,1,0:T(4,128)} %inverse_hbm.1, bf16[6,576,384]{2,1,0:T(8,128)(2,1)} %jac_hbm.1, s32[2,6]{1,0:T(2,128)} %bitcast.1, s32[1]{0:T(128)S(6)} %copy.9.load), custom_call_target="tpu_custom_call" | custom-call | tf_op jit(solution)/shard_map/pallas_call | solution.py:463
  34.1 1.5 %shard_map.87 = (f32[9,768]{1,0:T(8,128)}, f32[9,768]{1,0:T(8,128)}) custom-call(f32[9,768]{1,0:T(8,128)} %get-tuple-element.4.first, f32[9,768]{1,0:T(8,128)} %get-tuple-element.5.second), custom_call_target="tpu_custom_call" | custom-call | tf_op jit(solution)/shard_map/pallas_call | solution.py:445
where the time goes:
time: 35.8 us; the launch traced here: 35.6 us
  Pallas kernels  34.3 us (96%)
  between operations  1.29 us (4%)
    pallas_call x1, Pallas kernels, per_device(): pl.pallas_call(functools.partial(kernel, cells, grps), out_shape=(field,...  32.8 us
    pallas_call x1, Pallas kernels, finish(): pl.pallas_call(finish_kernel, out_shape=(shape, shape), in_specs=[vmem] *...  1.46 us

commit v1 on v0

v1 whole, which is shorter than its diff:
```python
import functools

import jax
import jax.numpy as jnp
from jax import lax
from jax.experimental import pallas as pl
from jax.experimental.pallas import tpu as pltpu
from jax.sharding import PartitionSpec as P

CAM_TILE = 64
REACH = 2
SPAN = 2 * REACH + 1
ORDER = sorted(range(-REACH, REACH + 1), key=abs)
LANES = 128
ROWS = 8
PACK = 32
NONE = -(1 << 20)
MESH = pl.DeviceIdType.MESH
F32 = jnp.float32
BF16 = jnp.bfloat16
I32 = jnp.int32


def round_up(value, step):
    return (value + step - 1) // step * step


def kernel(
    cells,
    grps,
    guess_hbm,
    right_hbm,
    blocks_hbm,
    inverse_hbm,
    jac_hbm,
    pattern_hbm,
    load_hbm,
    solution_ref,
    residual_ref,
    pattern,
    load,
    guess,
    right,
    blocks,
    inverse,
    jac,
    fields,
    keys,
    slot_send,
    slot_recv,
    scalar_send,
    scalar_recv,
    choose_slots,
    choose_field,
    choose_window,
    local_sem,
    jac_sem,
    field_send_sem,
    field_recv_sem,
    key_send_sem,
    key_recv_sem,
    slot_send_sem,
    slot_recv_sem,
    scalar_sem,
):
    params, cameras = guess.shape
    slots, rows_wide, points_wide = jac.shape
    tiles = cameras // CAM_TILE
    pairs = cameras // LANES
    coords = inverse.shape[0]
    point_tiles = inverse.shape[2] // LANES
    full = rows_wide // LANES
    slot_rows_sent = round_up(full * slots + slots // 2, 4)
    field_rows = full * tiles + tiles // 2
    field_rows_sent = round_up(field_rows, ROWS)
    field_pack = fields.shape[2]
    near_count = SPAN * grps
    close_count = 3 * grps
    devices = cells * grps
    cell = lax.axis_index("cell")
    grp = lax.axis_index("grp")

    def near(delta, turn):
        return (lax.rem(cell + delta + cells, cells), lax.rem(grp + turn + grps, grps))

    def slot_index(delta, turn):
        return ORDER.index(delta) * grps + turn % grps

    peers = sorted(
        [(d, t) for d in ORDER for t in range(grps) if (d, t) != (0, 0)],
        key=lambda peer: ((abs(peer[0]) + REACH) % (REACH + 1), -peer[1]),
    )
    first_wave = [(d, t) for d, t in peers if d == 0 or t == 0]
    second_wave = [(d, t) for d, t in peers if d != 0 and t != 0]
    key_index = {(0, 0): 0}
    for delta, turn in first_wave + second_wave:
        key_index[(delta, turn)] = len(key_index)

    turned = [lax.rem(grp + turn, grps) for turn in range(grps)]

    def everyone(act):
        for turn in range(1, grps):
            act(turn - 1, (cell, turned[turn]))

        def one_cell(delta, carry):
            other = lax.rem(cell + delta, cells)
            for turn in range(grps):
                act(delta * grps + (turn - 1), (other, turned[turn]))
            return carry

        lax.fori_loop(1, cells, one_cell, 0)

    barrier = pltpu.get_barrier_semaphore()

    def greet(index, device):
        pl.semaphore_signal(barrier, inc=1, device_id=device, device_id_type=MESH)

    if cells // 2 <= 2 * REACH:
        greeted = len(first_wave)
        for delta, turn in first_wave:
            greet(0, near(delta, turn))
    else:
        greeted = devices - 1
        everyone(greet)

    local = [
        pltpu.make_async_copy(src, dst, local_sem.at[i])
        for i, (src, dst) in enumerate(
            (
                (guess_hbm, guess),
                (pattern_hbm, pattern),
                (load_hbm, load),
                (blocks_hbm, blocks),
                (right_hbm, right),
                (inverse_hbm, inverse),
            )
        )
    ]
    jac_copies = [
        pltpu.make_async_copy(jac_hbm.at[s], jac.at[s], jac_sem.at[s]) for s in range(slots)
    ]
    for copy in local:
        copy.start()
    for copy in jac_copies:
        copy.start()

    def iota(shape, axis):
        return lax.broadcasted_iota(I32, shape, axis)

    def steps(value, width, count):
        return sum((value >= width * j).astype(I32) for j in range(1, count + 1))

    lane8 = iota((ROWS, LANES), 1)
    row8 = iota((ROWS, LANES), 0)
    low8 = lane8 < CAM_TILE
    low1 = iota((1, LANES), 1) < CAM_TILE
    even8 = lax.bitwise_and(row8, 1) == 0

    fields[:, :, field_rows_sent:, :] = jnp.zeros(
        (fields.shape[0], 3, field_pack - field_rows_sent, LANES), BF16
    )
    slot_recv[:, :, slot_rows_sent:, :] = jnp.zeros(
        (3, near_count, PACK - slot_rows_sent, LANES), BF16
    )

    pick_row = iota((field_pack, LANES), 0)
    pick_chunk = steps(pick_row, tiles, full)
    pick_tile = pick_row - pick_chunk * tiles
    pick_tail = pick_chunk == full
    source_low = 16 * pick_tile + 2 * pick_chunk
    other_tile = jnp.where(pick_tail, pick_tile + tiles // 2, pick_tile)
    flipped = other_tile + 1 - 2 * lax.bitwise_and(other_tile, 1)
    source_high = 16 * flipped + jnp.where(pick_tail, 2 * full, 2 * pick_chunk + 1)
    unused = pick_row >= field_rows
    source_low = jnp.where(unused, -1, source_low)
    source_high = jnp.where(unused, -1, source_high)
    picked_width = 16 * tiles
    lane_pick = iota((field_pack, LANES), 1)

    def one_hot(source):
        parts = [
            (source == lane_pick + LANES * j).astype(F32)
            for j in range(round_up(picked_width, LANES) // LANES)
        ]
        return jnp.concatenate(parts, axis=1)[:, :picked_width].astype(BF16)

    spread = jnp.concatenate([one_hot(source_low), one_hot(source_high)], axis=0)

    def to_rows(field):
        tall = jnp.concatenate([field, jnp.zeros((16 - params, cameras), F32)], axis=0)
        parts = []
        for i in range(pairs):
            block = tall[:, i * LANES : (i + 1) * LANES]
            parts += [block.astype(BF16), pltpu.roll(block, CAM_TILE, 1).astype(BF16)]
        both = jnp.dot(spread, jnp.concatenate(parts, axis=0), preferred_element_type=F32)
        low = lane_pick < CAM_TILE
        picked = jnp.where(low, both[:field_pack], both[field_pack:])
        return picked[:field_rows_sent].astype(BF16)

    def put_field(f, field):
        fields[f, 2, :field_rows_sent] = to_rows(field)

    def field_copies(f):
        return [
            pltpu.make_async_remote_copy(
                src_ref=fields.at[f, 2, pl.ds(0, field_rows_sent)],
                dst_ref=fields.at[f, side, pl.ds(0, field_rows_sent)],
                send_sem=field_send_sem.at[f],
                recv_sem=field_recv_sem.at[f],
                device_id=near(delta, 0),
                device_id_type=MESH,
            )
            for side, delta in ((0, 1), (1, -1))
        ]

    def wait_bytes(ref, sem):
        pltpu.make_async_copy(ref, ref, sem).wait()

    def field_bytes(f, sem):
        wait_bytes(fields.at[f, pl.ds(0, 2), pl.ds(0, field_rows_sent)], sem.at[f])

    local[0].wait()
    put_field(0, guess[...])

    local[1].wait()
    local[2].wait()
    live = [s < load[0] for s in range(slots)]
    ids = [pattern[0, s] for s in range(slots)]
    point_ids = [pattern[1, s] for s in range(slots)]
    live_rows = jnp.zeros((ROWS, LANES), I32)
    id_rows = jnp.full((ROWS, LANES), NONE, I32)
    point_rows = jnp.full((ROWS, LANES), -1, I32)
    first_rows = jnp.zeros((ROWS, LANES), F32)
    for s in range(slots):
        here = row8 == s
        id_rows = jnp.where(here, jnp.where(live[s], 8 * ids[s], NONE), id_rows)
        point_rows = jnp.where(here, point_ids[s], point_rows)
        live_rows = jnp.where(here, jnp.where(live[s], 1, 0), live_rows)
        first = live[s]
        for u in range(s):
            same = jnp.logical_and(live[u], point_ids[u] == point_ids[s])
            first = jnp.logical_and(first, jnp.logical_not(same))
        first_rows = jnp.where(here, jnp.where(first, 1.0, 0.0), first_rows)
    live8 = live_rows > 0
    shared = [
        jnp.logical_and(point_rows == point_ids[s], jnp.where(live[s], 1, 0) > 0)
        for s in range(slots)
    ]

    key_lane = lax.bitwise_and(iota((2, LANES), 1), PACK - 1)
    key_chunk = steps(key_lane, slots, full)
    key_slot = key_lane - slots * key_chunk
    key_row = iota((2, LANES), 0)
    key_tail = jnp.logical_and(key_chunk == full, key_slot < slots // 2)
    own_key = jnp.full((2, LANES), NONE, I32)
    for s in range(slots):
        code = jnp.where(live[s], 8 * ids[s], NONE)
        head = jnp.logical_and(jnp.logical_and(key_chunk < full, key_slot == s), key_row == 0)
        tail_row, tail_slot = divmod(s, slots // 2)
        tail = jnp.logical_and(
            jnp.logical_and(key_tail, key_slot == tail_slot), key_row == tail_row
        )
        own_key = jnp.where(head, code + key_chunk, own_key)
        own_key = jnp.where(tail, code + full + tail_row, own_key)
    keys[0] = own_key

    row_keys = [id_rows + b for b in range(full + 2)]

    window_lane = iota((1, LANES), 1)
    window_parts = [[], []]
    window_width = 3 * field_pack
    for group in range(round_up(window_width, LANES) // LANES):
        position = window_lane + LANES * group
        place = steps(position, field_pack, 2)
        side = jnp.where(place == 0, 0, jnp.where(place == 1, 2, 1))
        row = position - place * field_pack
        chunk = steps(row, tiles, full)
        tile = side * tiles + row - chunk * tiles
        off = row >= field_rows
        tail = jnp.logical_and(chunk == full, jnp.logical_not(off))
        window_parts[0].append(jnp.where(off, -1, 8 * tile + chunk))
        window_parts[1].append(jnp.where(tail, 8 * (tile + tiles // 2) + full + 1, -1))
    window_low = window_parts[0]
    window_high = window_parts[1]

    def matches(low_keys, high_keys):
        parts = []
        for b in range(full + 2):
            found = low_keys if b <= full else high_keys
            parts.append(
                jnp.concatenate([(key == row_keys[b]).astype(F32) for key in found], axis=1)
            )
        return jnp.concatenate(parts, axis=0).astype(BF16)

    choose_window[...] = matches(window_low, window_high)[:, :window_width]

    def slot_fields(chosen, rows):
        found = jnp.dot(chosen, rows, preferred_element_type=F32)
        parts = [found[b * ROWS : (b + 1) * ROWS] for b in range(full + 2)]
        tail = parts[full] + pltpu.roll(parts[full + 1], CAM_TILE, 1)
        return jnp.concatenate(parts[:full] + [tail], axis=1)[:, :rows_wide]

    def window_slots(f):
        return slot_fields(choose_window[...], fields[f].reshape(window_width, LANES))

    def block_product(field):
        total = blocks[0] * field[0:1, :]
        for k in range(1, params):
            total = total + blocks[k] * field[k : k + 1, :]
        return total

    local[3].wait()
    row_wide = iota((params, cameras), 0)
    diagonal = blocks[0]
    for k in range(1, params):
        diagonal = jnp.where(row_wide == k, blocks[k], diagonal)
    scale = 1.0 / diagonal
    local[4].wait()
    residual0 = right[...] - block_product(guess[...])
    put_field(1, residual0 * scale)
    put_field(2, scale)
    local[5].wait()
    inverse_rows = []
    for j in range(coords):
        for i in range(coords):
            picked = jnp.zeros((ROWS, LANES), F32)
            for q in range(point_tiles):
                picked = jnp.where(
                    point_rows == q, inverse[j, i : i + 1, q * LANES : (q + 1) * LANES], picked
                )
            inverse_rows.append(picked)

    for copy in jac_copies:
        copy.wait()
    pl.semaphore_wait(barrier, greeted)

    for copy in field_copies(0):
        copy.start()

    def send_keys(wave, sem):
        for delta, turn in wave:
            pltpu.make_async_remote_copy(
                src_ref=keys.at[0],
                dst_ref=keys.at[key_index[(-delta, -turn % grps)]],
                send_sem=key_send_sem.at[sem],
                recv_sem=key_recv_sem.at[sem],
                device_id=near(delta, turn),
                device_id_type=MESH,
            ).start()

    first_keys = pl.ds(1, len(first_wave))
    second_keys = pl.ds(1 + len(first_wave), len(second_wave))
    send_keys(first_wave, 0)
    for f in (1, 2):
        for copy in field_copies(f):
            copy.start()

    def slot_rows(values):
        values = jnp.where(live_wide, values, 0.0)
        sums = jnp.zeros((ROWS, points_wide), F32)
        for s in range(slots):
            spread_row = jnp.where(shared_wide[s], values[s : s + 1, :], 0.0)
            sums = sums + jnp.dot(spread_row.astype(BF16), jac[s], preferred_element_type=F32)
        solved = []
        for j in range(coords):
            total = inverse_rows[j * coords] * sums[:, :LANES]
            for i in range(1, coords):
                total = total + inverse_rows[j * coords + i] * sums[:, i * LANES : (i + 1) * LANES]
            solved.append(total)
        solved = jnp.concatenate(solved, axis=1).astype(BF16).astype(F32)
        return sums, solved

    def slot_message(solved):
        parts = [jnp.zeros((ROWS, LANES), F32) for _ in range(PACK // ROWS)]
        tails = []
        for s in range(slots):
            row = jnp.broadcast_to(solved[s : s + 1, :], (ROWS, points_wide)).astype(BF16)
            product = lax.dot_general(
                row, jac[s], (((1,), (1,)), ((), ())), preferred_element_type=F32
            )
            product = jnp.where(live[s], product, 0.0)
            for b in range(full):
                at, inside = divmod(b * slots + s, ROWS)
                parts[at] = jnp.where(
                    row8 == inside, product[:, b * LANES : (b + 1) * LANES], parts[at]
                )
            tails.append(product[:, full * LANES :])
        for i in range(slots // 2):
            at, inside = divmod(full * slots + i, ROWS)
            both = jnp.concatenate([tails[i], tails[i + slots // 2]], axis=1)
            parts[at] = jnp.where(row8 == inside, both, parts[at])
        return jnp.concatenate(parts, axis=0).astype(BF16)

    def energy_of(sums, solved):
        energy = sums * solved
        lanes = energy[:, :LANES]
        for i in range(1, coords):
            lanes = lanes + energy[:, i * LANES : (i + 1) * LANES]
        return jnp.sum(lanes * first_rows, axis=0, keepdims=True)

    live_wide = jnp.concatenate([live8] * (full + 1), axis=1)[:, :rows_wide]
    shared_wide = [
        jnp.concatenate([shared[s]] * (full + 1), axis=1)[:, :rows_wide] for s in range(slots)
    ]

    def send_slots(turn_no, message, reach):
        slot_send[turn_no] = message
        slot_recv[turn_no, 0] = message
        for delta, turn in peers:
            if abs(delta) <= reach:
                pltpu.make_async_remote_copy(
                    src_ref=slot_send.at[turn_no, pl.ds(0, slot_rows_sent)],
                    dst_ref=slot_recv.at[
                        turn_no, slot_index(-delta, -turn), pl.ds(0, slot_rows_sent)
                    ],
                    send_sem=slot_send_sem.at[turn_no],
                    recv_sem=slot_recv_sem.at[turn_no],
                    device_id=near(delta, turn),
                    device_id_type=MESH,
                ).start()

    def wait_slots(turn_no, count, sem):
        wait_bytes(
            slot_recv.at[turn_no, pl.ds(1, count - 1), pl.ds(0, slot_rows_sent)], sem.at[turn_no]
        )

    def received(turn_no, count):
        return slot_recv[turn_no, :count].reshape(count * PACK, LANES)

    def own_back(turn_no, count):
        width = count * PACK
        found = jnp.dot(
            choose_field[:, :width], received(turn_no, count), preferred_element_type=F32
        )
        parts = []
        for i in range(pairs):
            first = found[32 * i : 32 * i + 16]
            second = found[32 * i + 16 : 32 * i + 32]
            first_turned = pltpu.roll(first, CAM_TILE, 1)
            second_turned = pltpu.roll(second, CAM_TILE, 1)
            top = jnp.where(
                low8,
                jnp.where(even8, first[:ROWS], first_turned[:ROWS]),
                jnp.where(even8, second_turned[:ROWS], second[:ROWS]),
            )
            last = jnp.where(
                low1,
                first[ROWS : ROWS + 1] + first_turned[ROWS + 1 : ROWS + 2],
                second_turned[ROWS : ROWS + 1] + second[ROWS + 1 : ROWS + 2],
            )
            parts.append(jnp.concatenate([top, last], axis=0))
        return jnp.concatenate(parts, axis=1)

    field_bytes(0, field_recv_sem)
    wait_bytes(keys.at[first_keys], key_recv_sem.at[0])
    send_keys(second_wave, 1)
    _, solved = slot_rows(window_slots(0))
    send_slots(0, slot_message(solved), REACH)

    wait_bytes(keys.at[second_keys], key_recv_sem.at[1])
    lows, highs = [], []
    place_lane = lax.shift_right_logical(window_lane, 5)
    per_group = LANES // PACK
    order = [(delta, turn) for delta in ORDER for turn in range(grps)]
    for group in range(near_count // per_group):
        low = jnp.full((1, LANES), NONE, I32)
        high = jnp.full((1, LANES), NONE, I32)
        for j in range(per_group):
            delta, turn = order[group * per_group + j]
            key = keys[key_index[(delta, turn)]] + 8 * tiles * delta
            low = jnp.where(place_lane == j, key[0:1], low)
            high = jnp.where(place_lane == j, key[1:2], high)
        lows.append(low)
        highs.append(high)
    choose_slots[...] = matches(lows, highs)
    half_row = lax.shift_right_logical(row8, 1)
    mixed = [jnp.where(row8 == 0, low, high) for low, high in zip(lows, highs)]
    for t in range(tiles):
        base = 8 * (tiles + t)
        top = jnp.concatenate([(low == base + half_row).astype(F32) for low in lows], axis=1)
        tail_key = jnp.where(row8 < 2, base + full + row8, -1)
        tail = jnp.concatenate([(mix == tail_key).astype(F32) for mix in mixed], axis=1)
        choose_field[16 * t : 16 * (t + 1)] = jnp.concatenate([top, tail], axis=0).astype(BF16)
    for f in (1, 2):
        field_bytes(f, field_recv_sem)
    start_slots = window_slots(1)
    scale_slots = window_slots(2)

    wait_slots(0, near_count, slot_recv_sem)
    back = slot_fields(choose_slots[...], received(0, near_count))
    direction_slots = start_slots + scale_slots * back
    _, solved = slot_rows(direction_slots)
    send_slots(1, slot_message(solved), REACH)
    field_bytes(1, field_send_sem)
    residual0 = residual0 + own_back(0, near_count)
    direction = residual0 * scale
    product1 = block_product(direction)
    put_field(3, (product1 - diagonal * direction) * scale)
    for copy in field_copies(3):
        copy.start()
    field_bytes(3, field_recv_sem)
    change_slots = window_slots(3)

    wait_slots(1, near_count, slot_recv_sem)
    back = slot_fields(choose_slots[...], received(1, near_count))
    sums, solved = slot_rows(scale_slots * back - change_slots)
    send_slots(2, slot_message(solved), 1)
    field_bytes(2, field_send_sem)
    energy = energy_of(sums, solved)
    image1 = product1 - own_back(1, near_count)
    trial = residual0 - image1
    shaped = trial * scale
    product2 = block_product(shaped)

    def lane_sum(field):
        total = field[:, :LANES]
        for i in range(1, pairs):
            total = total + field[:, i * LANES : (i + 1) * LANES]
        return jnp.sum(total, axis=0, keepdims=True) * (1.0 / grps)

    sums = jnp.zeros((ROWS, LANES), F32)
    for i, value in enumerate(
        (
            lane_sum(residual0 * direction),
            lane_sum(direction * image1),
            lane_sum(residual0 * shaped),
            lane_sum(trial * shaped),
            lane_sum(image1 * shaped),
            lane_sum(shaped * product2) - energy,
        )
    ):
        sums = jnp.where(row8 == i, value, sums)
    sums = jnp.sum(sums, axis=1, keepdims=True)
    own_sums = jnp.sum(jnp.where(row8 == lane8, sums, 0.0), axis=0, keepdims=True)
    scalar_send[...] = own_sums

    def send_scalars(index, device):
        pltpu.make_async_remote_copy(
            src_ref=scalar_send,
            dst_ref=scalar_recv.at[index],
            send_sem=scalar_sem.at[0],
            recv_sem=scalar_sem.at[1],
            device_id=device,
            device_id_type=MESH,
        ).start()

    everyone(send_scalars)

    wait_slots(2, close_count, slot_recv_sem)
    image2 = product2 - own_back(2, close_count)
    wait_bytes(scalar_recv, scalar_sem.at[1])
    totals = own_sums + jnp.sum(scalar_recv[...], axis=0)
    rz0, curve1, cross, trial_rz, mixed_sum, curve_w = [totals[:, i : i + 1] for i in range(6)]
    step1 = rz0 / curve1
    short = 1.0 - step1
    rz1 = short * short * rz0 + 2.0 * short * step1 * cross + step1 * step1 * trial_rz
    keep = short + rz1 / rz0
    curve2 = keep * keep * curve1 + 2.0 * keep * step1 * mixed_sum + step1 * step1 * curve_w
    step2 = rz1 / curve2
    near_part = step1 + step2 * keep
    far_part = step2 * step1
    solution_ref[...] = guess[...] + near_part * direction + far_part * shaped
    residual_ref[...] = residual0 - near_part * image1 - far_part * image2

    wait_bytes(scalar_recv, scalar_sem.at[0])
    for f in (0, 3):
        field_bytes(f, field_send_sem)
    wait_bytes(keys.at[first_keys], key_send_sem.at[0])
    wait_bytes(keys.at[second_keys], key_send_sem.at[1])
    for turn_no, count in enumerate((near_count, near_count, close_count)):
        wait_slots(turn_no, count, slot_send_sem)


def finish_kernel(first, second, solution_ref, residual_ref):
    solution_ref[...] = first[...]
    residual_ref[...] = second[...]


def finish(first, second):
    vmem = pl.BlockSpec(memory_space=pltpu.VMEM)
    shape = jax.ShapeDtypeStruct(first.shape, first.dtype)
    return pl.pallas_call(
        finish_kernel, out_shape=(shape, shape), in_specs=[vmem] * 2, out_specs=(vmem, vmem)
    )(*[pltpu.with_memory_space_constraint(x, pltpu.VMEM) for x in (first, second)])


def per_device(
    cells, grps, initial_guess, right_side, camera_blocks, point_inverse, jacobian_tiles, tile_pattern, cell_load
):
    params, cameras = initial_guess.shape
    slots, rows_wide, points_wide = jacobian_tiles.shape
    near = SPAN * grps
    tiles = cameras // CAM_TILE
    full = rows_wide // LANES
    field_pack = round_up(full * tiles + tiles // 2, 64)
    hbm = pl.BlockSpec(memory_space=pltpu.HBM)
    vmem = pl.BlockSpec(memory_space=pltpu.VMEM)
    dma = pltpu.SemaphoreType.DMA
    field = pltpu.VMEM((params, cameras), F32)
    first, second = pl.pallas_call(
        functools.partial(kernel, cells, grps),
        out_shape=(field, field),
        in_specs=[hbm] * 7,
        out_specs=(vmem, vmem),
        scratch_shapes=[
            pltpu.SMEM((2, slots), I32),
            pltpu.SMEM((1,), I32),
            pltpu.VMEM((params, cameras), F32),
            pltpu.VMEM((params, cameras), F32),
            pltpu.VMEM(camera_blocks.shape, F32),
            pltpu.VMEM(point_inverse.shape, F32),
            pltpu.VMEM(jacobian_tiles.shape, BF16),
            pltpu.VMEM((4, 3, field_pack, LANES), BF16),
            pltpu.VMEM((near, 2, LANES), I32),
            pltpu.VMEM((3, PACK, LANES), BF16),
            pltpu.VMEM((3, near, PACK, LANES), BF16),
            pltpu.VMEM((1, LANES), F32),
            pltpu.VMEM((cells * grps - 1, 1, LANES), F32),
            pltpu.VMEM((ROWS * (full + 2), near * PACK), BF16),
            pltpu.VMEM((16 * tiles, near * PACK), BF16),
            pltpu.VMEM((ROWS * (full + 2), 3 * field_pack), BF16),
            dma((6,)),
            dma((slots,)),
            dma((4,)),
            dma((4,)),
            dma((2,)),
            dma((2,)),
            dma((3,)),
            dma((3,)),
            dma((2,)),
        ],
        compiler_params=pltpu.CompilerParams(collective_id=0, has_side_effects=True),
    )(initial_guess, right_side, camera_blocks, point_inverse, jacobian_tiles, tile_pattern.T, cell_load)
    return finish(first, second)


def solution(mesh):
    placed = (
        P(None, "cell"),
        P(None, "cell"),
        P(None, None, "cell"),
        P(None, None, ("cell", "grp")),
        P(("cell", "grp"), None, None),
        P(("cell", "grp"), None),
        P("cell"),
    )
    return jax.shard_map(
        functools.partial(per_device, mesh.shape["cell"], mesh.shape["grp"]),
        mesh=mesh,
        in_specs=placed,
        out_specs=(P(None, "cell"), P(None, "cell")),
        check_vma=False,
    )
```

time: 35.8 us -> 32.8 us (0.916)
  Pallas kernels: 34.3 us -> 31.3 us
    pallas_call x1, Pallas kernels: 32.8 us -> 30.7 us  [per_device(): pl.pallas_call(functools.partial(kernel, cells, grps), out_shape=(field,...]
    pallas_call x1, Pallas kernels: 1.46 us -> 0.64 us  [finish(): pl.pallas_call(finish_kernel, out_shape=(shape, shape), in_specs=[vmem] *...]
where the time goes in v1:
time: 32.8 us; the launch traced here: 32.6 us
  Pallas kernels  31.3 us (95%)
  between operations  1.29 us (4%)
    pallas_call x1, Pallas kernels, per_device(): pl.pallas_call(functools.partial(kernel, cells, grps), out_shape=(field,...  30.7 us

profile of v1, /device:TPU:0, one launch (start us, length us, event | category | flops | bytes accessed | tf_op | source)
XLA Modules:
  0.0 32.6 jit_solution(5321058021993460596)
XLA Ops:
  1.3 30.7 %shard_map.86 = (f32[9,768]{1,0:T(8,128)S(1)}, f32[9,768]{1,0:T(8,128)S(1)}) custom-call(f32[9,768]{1,0:T(8,128)} %guess_hbm.1, f32[9,768]{1,0:T(8,128)} %right_hbm.1, f32[9,9,768]{2,1,0:T(8,128)} %blocks_hbm.1, f32[3,3,512]{2,1,0:T(4,128)} %inverse_hbm.1, bf16[6,576,384]{2,1,0:T(8,128)(2,1)} %jac_hbm.1, s32[2,6]{1,0:T(2,128)} %bitcast.1, s32[1]{0:T(128)S(6)} %copy.9.load_hbm), custom_call_target="tpu_custom_call" | custom-call | tf_op jit(solution)/shard_map/pallas_call | solution.py:600
  32.0 0.6 %shard_map.87 = (f32[9,768]{1,0:T(8,128)}, f32[9,768]{1,0:T(8,128)}) custom-call(f32[9,768]{1,0:T(8,128)S(1)} %get-tuple-element.4.first, f32[9,768]{1,0:T(8,128)S(1)} %get-tuple-element.5.second), custom_call_target="tpu_custom_call" | custom-call | tf_op jit(solution)/shard_map/pallas_call | solution.py:582

commit v2 on v1

--- a/solution.py
+++ b/solution.py
@@ -488,26 +488,28 @@
 
     wait_slots(0, near_count, slot_recv_sem)
     back = slot_fields(choose_slots[...], received(0, near_count))
+    own_found = own_back(0, near_count)
     direction_slots = start_slots + scale_slots * back
     _, solved = slot_rows(direction_slots)
-    send_slots(1, slot_message(solved), REACH)
-    field_bytes(1, field_send_sem)
-    residual0 = residual0 + own_back(0, near_count)
+    residual0 = residual0 + own_found
     direction = residual0 * scale
     product1 = block_product(direction)
     put_field(3, (product1 - diagonal * direction) * scale)
     for copy in field_copies(3):
         copy.start()
+    field_bytes(1, field_send_sem)
+    send_slots(1, slot_message(solved), REACH)
     field_bytes(3, field_recv_sem)
     change_slots = window_slots(3)
 
     wait_slots(1, near_count, slot_recv_sem)
     back = slot_fields(choose_slots[...], received(1, near_count))
+    own_found = own_back(1, near_count)
     sums, solved = slot_rows(scale_slots * back - change_slots)
     send_slots(2, slot_message(solved), 1)
     field_bytes(2, field_send_sem)
     energy = energy_of(sums, solved)
-    image1 = product1 - own_back(1, near_count)
+    image1 = product1 - own_found
     trial = residual0 - image1
     shaped = trial * scale
     product2 = block_product(shaped)

time: 32.8 us -> 32 us (0.976)
  Pallas kernels: 31.3 us -> 30.5 us
    pallas_call x1, Pallas kernels: 30.7 us -> 29.9 us  [per_device(): pl.pallas_call(functools.partial(kernel, cells, grps), out_shape=(field,...]
where the time goes in v2:
time: 32 us; the launch traced here: 31.8 us
  Pallas kernels  30.5 us (95%)
  between operations  1.29 us (4%)
    pallas_call x1, Pallas kernels, per_device(): pl.pallas_call(functools.partial(kernel, cells, grps), out_shape=(field,...  29.9 us
    pallas_call x1, Pallas kernels, finish(): pl.pallas_call(finish_kernel, out_shape=(shape, shape), in_specs=[vmem] *...  0.64 us

profile of v2, /device:TPU:0, one launch (start us, length us, event | category | flops | bytes accessed | tf_op | source)
XLA Modules:
  0.0 31.8 jit_solution(9477747981230088757)
XLA Ops:
  1.3 29.9 %shard_map.86 = (f32[9,768]{1,0:T(8,128)S(1)}, f32[9,768]{1,0:T(8,128)S(1)}) custom-call(f32[9,768]{1,0:T(8,128)} %guess_hbm.1, f32[9,768]{1,0:T(8,128)} %right_hbm.1, f32[9,9,768]{2,1,0:T(8,128)} %blocks_hbm.1, f32[3,3,512]{2,1,0:T(4,128)} %inverse_hbm.1, bf16[6,576,384]{2,1,0:T(8,128)(2,1)} %jac_hbm.1, s32[2,6]{1,0:T(2,128)} %bitcast.1, s32[1]{0:T(128)S(6)} %copy.9.load_hbm), custom_call_target="tpu_custom_call" | custom-call | tf_op jit(solution)/shard_map/pallas_call | solution.py:602
  31.2 0.6 %shard_map.87 = (f32[9,768]{1,0:T(8,128)}, f32[9,768]{1,0:T(8,128)}) custom-call(f32[9,768]{1,0:T(8,128)S(1)} %get-tuple-element.4.first, f32[9,768]{1,0:T(8,128)S(1)} %get-tuple-element.5.second), custom_call_target="tpu_custom_call" | custom-call | tf_op jit(solution)/shard_map/pallas_call | solution.py:584

commit v3 on v2

--- a/solution.py
+++ b/solution.py
@@ -44,6 +44,7 @@
     blocks,
     inverse,
     jac,
+    jac_turned,
     fields,
     keys,
     slot_send,
@@ -354,6 +355,8 @@
     for f in (1, 2):
         for copy in field_copies(f):
             copy.start()
+    for s in range(slots):
+        jac_turned[s] = jac[s].T
 
     def slot_rows(values):
         values = jnp.where(live_wide, values, 0.0)
@@ -375,9 +378,7 @@
         tails = []
         for s in range(slots):
             row = jnp.broadcast_to(solved[s : s + 1, :], (ROWS, points_wide)).astype(BF16)
-            product = lax.dot_general(
-                row, jac[s], (((1,), (1,)), ((), ())), preferred_element_type=F32
-            )
+            product = jnp.dot(row, jac_turned[s], preferred_element_type=F32)
             product = jnp.where(live[s], product, 0.0)
             for b in range(full):
                 at, inside = divmod(b * slots + s, ROWS)
@@ -432,21 +433,21 @@
         found = jnp.dot(
             choose_field[:, :width], received(turn_no, count), preferred_element_type=F32
         )
+        tail_low = found[ROWS * tiles : ROWS * tiles + 16]
+        tail_high = found[ROWS * tiles + 16 : ROWS * tiles + 32]
+        lasts_low = tail_low + pltpu.roll(tail_high, CAM_TILE, 1)
+        lasts_high = pltpu.roll(tail_low, CAM_TILE, 1) + tail_high
         parts = []
         for i in range(pairs):
-            first = found[32 * i : 32 * i + 16]
-            second = found[32 * i + 16 : 32 * i + 32]
-            first_turned = pltpu.roll(first, CAM_TILE, 1)
-            second_turned = pltpu.roll(second, CAM_TILE, 1)
+            first = found[2 * ROWS * i : 2 * ROWS * i + ROWS]
+            second = found[2 * ROWS * i + ROWS : 2 * ROWS * (i + 1)]
             top = jnp.where(
                 low8,
-                jnp.where(even8, first[:ROWS], first_turned[:ROWS]),
-                jnp.where(even8, second_turned[:ROWS], second[:ROWS]),
+                jnp.where(even8, first, pltpu.roll(first, CAM_TILE, 1)),
+                jnp.where(even8, pltpu.roll(second, CAM_TILE, 1), second),
             )
             last = jnp.where(
-                low1,
-                first[ROWS : ROWS + 1] + first_turned[ROWS + 1 : ROWS + 2],
-                second_turned[ROWS : ROWS + 1] + second[ROWS + 1 : ROWS + 2],
+                low1, lasts_low[2 * i : 2 * i + 1], lasts_high[2 * i + 1 : 2 * i + 2]
             )
             parts.append(jnp.concatenate([top, last], axis=0))
         return jnp.concatenate(parts, axis=1)
@@ -474,13 +475,16 @@
         highs.append(high)
     choose_slots[...] = matches(lows, highs)
     half_row = lax.shift_right_logical(row8, 1)
-    mixed = [jnp.where(row8 == 0, low, high) for low, high in zip(lows, highs)]
+    heads = []
     for t in range(tiles):
-        base = 8 * (tiles + t)
-        top = jnp.concatenate([(low == base + half_row).astype(F32) for low in lows], axis=1)
-        tail_key = jnp.where(row8 < 2, base + full + row8, -1)
-        tail = jnp.concatenate([(mix == tail_key).astype(F32) for mix in mixed], axis=1)
-        choose_field[16 * t : 16 * (t + 1)] = jnp.concatenate([top, tail], axis=0).astype(BF16)
+        key = 8 * (tiles + t) + half_row
+        heads.append(jnp.concatenate([(low == key).astype(F32) for low in lows], axis=1))
+    tails = []
+    for kind, found in ((full, lows), (full + 1, highs)):
+        for at in (0, ROWS):
+            key = jnp.where(row8 + at < tiles, 8 * (tiles + at + row8) + kind, -1)
+            tails.append(jnp.concatenate([(lane == key).astype(F32) for lane in found], axis=1))
+    choose_field[...] = jnp.concatenate(heads + tails, axis=0).astype(BF16)
     for f in (1, 2):
         field_bytes(f, field_recv_sem)
     start_slots = window_slots(1)
@@ -573,16 +577,27 @@
         wait_slots(turn_no, count, slot_send_sem)
 
 
-def finish_kernel(first, second, solution_ref, residual_ref):
-    solution_ref[...] = first[...]
-    residual_ref[...] = second[...]
+def finish_kernel(first, second, solution_ref, residual_ref, sem):
+    copies = [
+        pltpu.make_async_copy(first, solution_ref, sem.at[0]),
+        pltpu.make_async_copy(second, residual_ref, sem.at[1]),
+    ]
+    for copy in copies:
+        copy.start()
+    for copy in copies:
+        copy.wait()
 
 
 def finish(first, second):
     vmem = pl.BlockSpec(memory_space=pltpu.VMEM)
+    hbm = pl.BlockSpec(memory_space=pltpu.HBM)
     shape = jax.ShapeDtypeStruct(first.shape, first.dtype)
     return pl.pallas_call(
-        finish_kernel, out_shape=(shape, shape), in_specs=[vmem] * 2, out_specs=(vmem, vmem)
+        finish_kernel,
+        out_shape=(shape, shape),
+        in_specs=[vmem] * 2,
+        out_specs=(hbm, hbm),
+        scratch_shapes=[pltpu.SemaphoreType.DMA((2,))],
     )(*[pltpu.with_memory_space_constraint(x, pltpu.VMEM) for x in (first, second)])
 
 
@@ -612,6 +627,7 @@
             pltpu.VMEM(camera_blocks.shape, F32),
             pltpu.VMEM(point_inverse.shape, F32),
             pltpu.VMEM(jacobian_tiles.shape, BF16),
+            pltpu.VMEM((slots, points_wide, rows_wide), BF16),
             pltpu.VMEM((4, 3, field_pack, LANES), BF16),
             pltpu.VMEM((near, 2, LANES), I32),
             pltpu.VMEM((3, PACK, LANES), BF16),
@@ -619,7 +635,7 @@
             pltpu.VMEM((1, LANES), F32),
             pltpu.VMEM((cells * grps - 1, 1, LANES), F32),
             pltpu.VMEM((ROWS * (full + 2), near * PACK), BF16),
-            pltpu.VMEM((16 * tiles, near * PACK), BF16),
+            pltpu.VMEM((ROWS * tiles + 32, near * PACK), BF16),
             pltpu.VMEM((ROWS * (full + 2), 3 * field_pack), BF16),
             dma((6,)),
             dma((slots,)),

time: 32 us -> 31.3 us (0.978)
  Pallas kernels: 30.5 us -> 29.9 us
    pallas_call x1, Pallas kernels: 29.9 us -> 29.2 us  [per_device(): pl.pallas_call(functools.partial(kernel, cells, grps), out_shape=(field,...]
where the time goes in v3:
time: 31.3 us; the launch traced here: 31.2 us
  Pallas kernels  29.9 us (96%)
  between operations  1.29 us (4%)
    pallas_call x1, Pallas kernels, per_device(): pl.pallas_call(functools.partial(kernel, cells, grps), out_shape=(field,...  29.2 us
    pallas_call x1, Pallas kernels, finish(): pl.pallas_call(finish_kernel, out_shape=(shape, shape), in_specs=[vmem] *...  0.66 us

profile of v3, /device:TPU:0, one launch (start us, length us, event | category | flops | bytes accessed | tf_op | source)
XLA Modules:
  0.0 31.2 jit_solution(13516611497084528727)
XLA Ops:
  1.3 29.2 %shard_map.86 = (f32[9,768]{1,0:T(8,128)S(1)}, f32[9,768]{1,0:T(8,128)S(1)}) custom-call(f32[9,768]{1,0:T(8,128)} %guess_hbm.1, f32[9,768]{1,0:T(8,128)} %right_hbm.1, f32[9,9,768]{2,1,0:T(8,128)} %blocks_hbm.1, f32[3,3,512]{2,1,0:T(4,128)} %inverse_hbm.1, bf16[6,576,384]{2,1,0:T(8,128)(2,1)} %jac_hbm.1, s32[2,6]{1,0:T(2,128)} %bitcast.1, s32[1]{0:T(128)S(6)} %copy.9.load_hbm), custom_call_target="tpu_custom_call" | custom-call | tf_op jit(solution)/shard_map/pallas_call | solution.py:617
  30.5 0.7 %shard_map.87 = (f32[9,768]{1,0:T(8,128)}, f32[9,768]{1,0:T(8,128)}) custom-call(f32[9,768]{1,0:T(8,128)S(1)} %get-tuple-element.4.first, f32[9,768]{1,0:T(8,128)S(1)} %get-tuple-element.5.second), custom_call_target="tpu_custom_call" | custom-call | tf_op jit(solution)/shard_map/pallas_call | solution.py:595

commit v4 on v3

--- a/solution.py
+++ b/solution.py
@@ -45,6 +45,7 @@
     inverse,
     jac,
     jac_turned,
+    jac_tails,
     fields,
     keys,
     slot_send,
@@ -355,15 +356,30 @@
     for f in (1, 2):
         for copy in field_copies(f):
             copy.start()
+    wide = full * LANES
     for s in range(slots):
-        jac_turned[s] = jac[s].T
+        jac_turned[s] = jac[s, :wide].T
+    for i in range(slots // 2):
+        both = jnp.concatenate([jac[i, wide:], jac[i + slots // 2, wide:]], axis=0)
+        jac_tails[i] = both.T
 
     def slot_rows(values):
         values = jnp.where(live_wide, values, 0.0)
         sums = jnp.zeros((ROWS, points_wide), F32)
+        rests = []
         for s in range(slots):
             spread_row = jnp.where(shared_wide[s], values[s : s + 1, :], 0.0)
-            sums = sums + jnp.dot(spread_row.astype(BF16), jac[s], preferred_element_type=F32)
+            low_row = spread_row.astype(BF16)
+            rests.append(low_row[:, full * LANES :])
+            sums = sums + jnp.dot(
+                low_row[:, : full * LANES], jac[s, : full * LANES], preferred_element_type=F32
+            )
+        rest = jnp.concatenate(rests, axis=1)
+        sums = sums + jnp.dot(
+            rest,
+            jnp.concatenate([jac[s, full * LANES :] for s in range(slots)], axis=0),
+            preferred_element_type=F32,
+        )
         solved = []
         for j in range(coords):
             total = inverse_rows[j * coords] * sums[:, :LANES]
@@ -375,7 +391,6 @@
 
     def slot_message(solved):
         parts = [jnp.zeros((ROWS, LANES), F32) for _ in range(PACK // ROWS)]
-        tails = []
         for s in range(slots):
             row = jnp.broadcast_to(solved[s : s + 1, :], (ROWS, points_wide)).astype(BF16)
             product = jnp.dot(row, jac_turned[s], preferred_element_type=F32)
@@ -385,10 +400,13 @@
                 parts[at] = jnp.where(
                     row8 == inside, product[:, b * LANES : (b + 1) * LANES], parts[at]
                 )
-            tails.append(product[:, full * LANES :])
+        short = solved.astype(BF16)
         for i in range(slots // 2):
             at, inside = divmod(full * slots + i, ROWS)
-            both = jnp.concatenate([tails[i], tails[i + slots // 2]], axis=1)
+            product = jnp.dot(short, jac_tails[i], preferred_element_type=F32)
+            product = jnp.where(live8, product, 0.0)
+            other = i + slots // 2
+            both = jnp.where(low1, product[i : i + 1], product[other : other + 1])
             parts[at] = jnp.where(row8 == inside, both, parts[at])
         return jnp.concatenate(parts, axis=0).astype(BF16)
 
@@ -627,7 +645,8 @@
             pltpu.VMEM(camera_blocks.shape, F32),
             pltpu.VMEM(point_inverse.shape, F32),
             pltpu.VMEM(jacobian_tiles.shape, BF16),
-            pltpu.VMEM((slots, points_wide, rows_wide), BF16),
+            pltpu.VMEM((slots, points_wide, full * LANES), BF16),
+            pltpu.VMEM((slots // 2, points_wide, LANES), BF16),
             pltpu.VMEM((4, 3, field_pack, LANES), BF16),
             pltpu.VMEM((near, 2, LANES), I32),
             pltpu.VMEM((3, PACK, LANES), BF16),

time: 31.3 us -> 30.9 us (0.987)
  Pallas kernels: 29.9 us -> 29.5 us
    pallas_call x1, Pallas kernels: 29.2 us -> 28.8 us  [per_device(): pl.pallas_call(functools.partial(kernel, cells, grps), out_shape=(field,...]
where the time goes in v4:
time: 30.9 us; the launch traced here: 30.7 us
  Pallas kernels  29.5 us (95%)
  between operations  1.29 us (4%)
    pallas_call x1, Pallas kernels, per_device(): pl.pallas_call(functools.partial(kernel, cells, grps), out_shape=(field,...  28.8 us
    pallas_call x1, Pallas kernels, finish(): pl.pallas_call(finish_kernel, out_shape=(shape, shape), in_specs=[vmem] *...  0.66 us

profile of v4, /device:TPU:0, one launch (start us, length us, event | category | flops | bytes accessed | tf_op | source)
XLA Modules:
  0.0 30.7 jit_solution(10914067660008417627)
XLA Ops:
  1.3 28.8 %shard_map.86 = (f32[9,768]{1,0:T(8,128)S(1)}, f32[9,768]{1,0:T(8,128)S(1)}) custom-call(f32[9,768]{1,0:T(8,128)} %guess_hbm.1, f32[9,768]{1,0:T(8,128)} %right_hbm.1, f32[9,9,768]{2,1,0:T(8,128)} %blocks_hbm.1, f32[3,3,512]{2,1,0:T(4,128)} %inverse_hbm.1, bf16[6,576,384]{2,1,0:T(8,128)(2,1)} %jac_hbm.1, s32[2,6]{1,0:T(2,128)} %bitcast.1, s32[1]{0:T(128)S(6)} %copy.9.load_hbm), custom_call_target="tpu_custom_call" | custom-call | tf_op jit(solution)/shard_map/pallas_call | solution.py:635
  30.1 0.7 %shard_map.87 = (f32[9,768]{1,0:T(8,128)}, f32[9,768]{1,0:T(8,128)}) custom-call(f32[9,768]{1,0:T(8,128)S(1)} %get-tuple-element.4.first, f32[9,768]{1,0:T(8,128)S(1)} %get-tuple-element.5.second), custom_call_target="tpu_custom_call" | custom-call | tf_op jit(solution)/shard_map/pallas_call | solution.py:613

commit v5 on v4

--- a/solution.py
+++ b/solution.py
@@ -359,25 +359,36 @@
     wide = full * LANES
     for s in range(slots):
         jac_turned[s] = jac[s, :wide].T
+    spare = jac_tails.shape[1] - slots // 2 * LANES
+    if spare:
+        jac_tails[:, slots // 2 * LANES :] = jnp.zeros((points_wide, spare), BF16)
     for i in range(slots // 2):
         both = jnp.concatenate([jac[i, wide:], jac[i + slots // 2, wide:]], axis=0)
-        jac_tails[i] = both.T
+        jac_tails[:, i * LANES : (i + 1) * LANES] = both.T
 
     def slot_rows(values):
         values = jnp.where(live_wide, values, 0.0)
-        sums = jnp.zeros((ROWS, points_wide), F32)
-        rests = []
-        for s in range(slots):
-            spread_row = jnp.where(shared_wide[s], values[s : s + 1, :], 0.0)
-            low_row = spread_row.astype(BF16)
-            rests.append(low_row[:, full * LANES :])
-            sums = sums + jnp.dot(
-                low_row[:, : full * LANES], jac[s, : full * LANES], preferred_element_type=F32
+        half = slots // 2
+        wide = full * LANES
+        split = points_wide // (2 * LANES) * (2 * LANES)
+        rows = [jnp.where(shared_wide[s], values[s : s + 1, :], 0.0) for s in range(slots)]
+        left = jnp.zeros((ROWS, split), F32)
+        right = jnp.zeros((ROWS, points_wide - split), F32)
+        for i in range(half):
+            u = i + half
+            both = jnp.concatenate([rows[i][:, :wide], rows[u][:, :wide]], axis=0).astype(BF16)
+            found = jnp.dot(
+                both,
+                jnp.concatenate([jac[i, :wide], jac[u, :wide]], axis=1),
+                preferred_element_type=F32,
             )
-        rest = jnp.concatenate(rests, axis=1)
-        sums = sums + jnp.dot(
+            total = found[:ROWS, :points_wide] + found[ROWS:, points_wide:]
+            left = left + total[:, :split]
+            right = right + total[:, split:]
+        rest = jnp.concatenate([row[:, wide:].astype(BF16) for row in rows], axis=1)
+        sums = jnp.concatenate([left, right], axis=1) + jnp.dot(
             rest,
-            jnp.concatenate([jac[s, full * LANES :] for s in range(slots)], axis=0),
+            jnp.concatenate([jac[s, wide:] for s in range(slots)], axis=0),
             preferred_element_type=F32,
         )
         solved = []
@@ -400,11 +411,10 @@
                 parts[at] = jnp.where(
                     row8 == inside, product[:, b * LANES : (b + 1) * LANES], parts[at]
                 )
-        short = solved.astype(BF16)
+        shorts = jnp.dot(solved.astype(BF16), jac_tails[...], preferred_element_type=F32)
         for i in range(slots // 2):
             at, inside = divmod(full * slots + i, ROWS)
-            product = jnp.dot(short, jac_tails[i], preferred_element_type=F32)
-            product = jnp.where(live8, product, 0.0)
+            product = jnp.where(live8, shorts[:, i * LANES : (i + 1) * LANES], 0.0)
             other = i + slots // 2
             both = jnp.where(low1, product[i : i + 1], product[other : other + 1])
             parts[at] = jnp.where(row8 == inside, both, parts[at])
@@ -646,7 +656,7 @@
             pltpu.VMEM(point_inverse.shape, F32),
             pltpu.VMEM(jacobian_tiles.shape, BF16),
             pltpu.VMEM((slots, points_wide, full * LANES), BF16),
-            pltpu.VMEM((slots // 2, points_wide, LANES), BF16),
+            pltpu.VMEM((points_wide, round_up(slots // 2, 2) * LANES), BF16),
             pltpu.VMEM((4, 3, field_pack, LANES), BF16),
             pltpu.VMEM((near, 2, LANES), I32),
             pltpu.VMEM((3, PACK, LANES), BF16),

time: 30.9 us -> 30.4 us (0.984)
  Pallas kernels: 29.5 us -> 28.9 us
    pallas_call x1, Pallas kernels: 28.8 us -> 28.3 us  [per_device(): pl.pallas_call(functools.partial(kernel, cells, grps), out_shape=(field,...]
where the time goes in v5:
time: 30.4 us; the launch traced here: 30.2 us
  Pallas kernels  28.9 us (95%)
  between operations  1.29 us (4%)
    pallas_call x1, Pallas kernels, per_device(): pl.pallas_call(functools.partial(kernel, cells, grps), out_shape=(field,...  28.3 us
    pallas_call x1, Pallas kernels, finish(): pl.pallas_call(finish_kernel, out_shape=(shape, shape), in_specs=[vmem] *...  0.66 us

profile of v5, /device:TPU:0, one launch (start us, length us, event | category | flops | bytes accessed | tf_op | source)
XLA Modules:
  0.0 30.2 jit_solution(5311941485679534024)
XLA Ops:
  1.3 28.3 %shard_map.86 = (f32[9,768]{1,0:T(8,128)S(1)}, f32[9,768]{1,0:T(8,128)S(1)}) custom-call(f32[9,768]{1,0:T(8,128)} %guess_hbm.1, f32[9,768]{1,0:T(8,128)} %right_hbm.1, f32[9,9,768]{2,1,0:T(8,128)} %blocks_hbm.1, f32[3,3,512]{2,1,0:T(4,128)} %inverse_hbm.1, bf16[6,576,384]{2,1,0:T(8,128)(2,1)} %jac_hbm.1, s32[2,6]{1,0:T(2,128)} %bitcast.1, s32[1]{0:T(128)S(6)} %copy.9.load_hbm), custom_call_target="tpu_custom_call" | custom-call | tf_op jit(solution)/shard_map/pallas_call | solution.py:645
  29.6 0.7 %shard_map.87 = (f32[9,768]{1,0:T(8,128)}, f32[9,768]{1,0:T(8,128)}) custom-call(f32[9,768]{1,0:T(8,128)S(1)} %get-tuple-element.4.first, f32[9,768]{1,0:T(8,128)S(1)} %get-tuple-element.5.second), custom_call_target="tpu_custom_call" | custom-call | tf_op jit(solution)/shard_map/pallas_call | solution.py:623

commit v6 on v5

--- a/solution.py
+++ b/solution.py
@@ -372,6 +372,12 @@
         wide = full * LANES
         split = points_wide // (2 * LANES) * (2 * LANES)
         rows = [jnp.where(shared_wide[s], values[s : s + 1, :], 0.0) for s in range(slots)]
+        rest = jnp.concatenate([row[:, wide:].astype(BF16) for row in rows], axis=1)
+        tail = jnp.dot(
+            rest,
+            jnp.concatenate([jac[s, wide:] for s in range(slots)], axis=0),
+            preferred_element_type=F32,
+        )
         left = jnp.zeros((ROWS, split), F32)
         right = jnp.zeros((ROWS, points_wide - split), F32)
         for i in range(half):
@@ -385,12 +391,7 @@
             total = found[:ROWS, :points_wide] + found[ROWS:, points_wide:]
             left = left + total[:, :split]
             right = right + total[:, split:]
-        rest = jnp.concatenate([row[:, wide:].astype(BF16) for row in rows], axis=1)
-        sums = jnp.concatenate([left, right], axis=1) + jnp.dot(
-            rest,
-            jnp.concatenate([jac[s, wide:] for s in range(slots)], axis=0),
-            preferred_element_type=F32,
-        )
+        sums = jnp.concatenate([left, right], axis=1) + tail
         solved = []
         for j in range(coords):
             total = inverse_rows[j * coords] * sums[:, :LANES]
@@ -482,8 +483,8 @@
 
     field_bytes(0, field_recv_sem)
     wait_bytes(keys.at[first_keys], key_recv_sem.at[0])
+    _, solved = slot_rows(window_slots(0))
     send_keys(second_wave, 1)
-    _, solved = slot_rows(window_slots(0))
     send_slots(0, slot_message(solved), REACH)
 
     wait_bytes(keys.at[second_keys], key_recv_sem.at[1])

time: 30.4 us -> 30.9 us (1.016)
  Pallas kernels: 28.9 us -> 29.5 us
    pallas_call x1, Pallas kernels: 28.3 us -> 28.8 us  [per_device(): pl.pallas_call(functools.partial(kernel, cells, grps), out_shape=(field,...]
where the time goes in v6:
time: 30.9 us; the launch traced here: 30.8 us
  Pallas kernels  29.5 us (95%)
  between operations  1.29 us (4%)
    pallas_call x1, Pallas kernels, per_device(): pl.pallas_call(functools.partial(kernel, cells, grps), out_shape=(field,...  28.8 us
    pallas_call x1, Pallas kernels, finish(): pl.pallas_call(finish_kernel, out_shape=(shape, shape), in_specs=[vmem] *...  0.66 us

profile of v6, /device:TPU:0, one launch (start us, length us, event | category | flops | bytes accessed | tf_op | source)
XLA Modules:
  0.0 30.8 jit_solution(7620589878975051627)
XLA Ops:
  1.3 28.8 %shard_map.86 = (f32[9,768]{1,0:T(8,128)S(1)}, f32[9,768]{1,0:T(8,128)S(1)}) custom-call(f32[9,768]{1,0:T(8,128)} %guess_hbm.1, f32[9,768]{1,0:T(8,128)} %right_hbm.1, f32[9,9,768]{2,1,0:T(8,128)} %blocks_hbm.1, f32[3,3,512]{2,1,0:T(4,128)} %inverse_hbm.1, bf16[6,576,384]{2,1,0:T(8,128)(2,1)} %jac_hbm.1, s32[2,6]{1,0:T(2,128)} %bitcast.1, s32[1]{0:T(128)S(6)} %copy.9.load_hbm), custom_call_target="tpu_custom_call" | custom-call | tf_op jit(solution)/shard_map/pallas_call | solution.py:646
  30.1 0.7 %shard_map.87 = (f32[9,768]{1,0:T(8,128)}, f32[9,768]{1,0:T(8,128)}) custom-call(f32[9,768]{1,0:T(8,128)S(1)} %get-tuple-element.4.first, f32[9,768]{1,0:T(8,128)S(1)} %get-tuple-element.5.second), custom_call_target="tpu_custom_call" | custom-call | tf_op jit(solution)/shard_map/pallas_call | solution.py:624
